TPU v7x, 32 devices: a whole 2x2x4 slice. The times are simulated.
32 devices in a mesh: grid: 16 (over z, y, x), col: 2 (over core).
Axes of the slice: x: 2, y: 2, z: 4, core: 2. Of those that a mesh axis runs over, the one named last changes fastest.
Arguments:
- orbitals: bfloat16 [884736, 256], P(('grid', 'col')), may hold values from -6 to 6
- points: int32 [1024], replicated, may hold values from 0 to 884735, as said below
- cinv: bfloat16 [1024, 256], replicated, may hold values from -0.1875 to 0.1875
Outputs:
- potential: bfloat16 [256, 884736], P(None, ('grid', 'col'))
- coupling: float32 [1024, 256], P(('grid', 'col'))
Inputs may be any that keep to these rules, and one draw needn't show every extreme that they name: `points`: 1024 distinct grid rows.
All inputs are finite; a program needn't handle non-finite values.
Results may differ from a plain program's by a relative error of at most 0.0046.
Values may be sent and summed in bfloat16 or wider, within the bound.
No kernel may reach another device: no remote copies, remote signals or barrier semaphores. Data moves between devices by JAX's collectives and lax.ppermute only.
A program may use at most 448 MiB of HBM per device.

v0:
```python
import functools
import math

import jax
import jax.numpy as jnp
import numpy as np
from jax import lax
from jax.experimental import pallas as pl
from jax.experimental.pallas import tpu as pltpu
from jax.sharding import PartitionSpec as P

NX = 96


screening = 0.25


def kernel_table(size):
    index = jnp.arange(size)
    wave = jnp.where(index < (size + 1) // 2, index, index - size).astype(jnp.float32) * (
        2.0 * math.pi / size
    )
    squared = wave[:, None, None] ** 2 + wave[None, :, None] ** 2 + wave[None, None, :] ** 2
    return jnp.where(squared > 0, 1.0 / (squared + screening), 0.0)


def along(table, values, axis):
    forms = {1: "kn,cnyz->ckyz", 2: "kn,cxnz->cxkz", 3: "kn,cxyn->cxyk"}
    return jnp.einsum(forms[axis], table, values, precision=lax.Precision.HIGHEST)


def screened_solve(field):
    size = field.shape[1]
    index = jnp.arange(size, dtype=jnp.int32)
    phase = index[:, None] * index[None, :] % size
    angle = phase.astype(jnp.float32) * (2.0 * math.pi / size)
    cos_table = jnp.cos(angle)
    sin_table = jnp.sin(angle)
    real_part = along(cos_table, field, 3)
    imag_part = -along(sin_table, field, 3)
    for axis in (2, 1):
        real_part, imag_part = (
            along(cos_table, real_part, axis) + along(sin_table, imag_part, axis),
            along(cos_table, imag_part, axis) - along(sin_table, real_part, axis),
        )
    weights = kernel_table(size)
    real_part = real_part * weights
    imag_part = imag_part * weights
    for axis in (1, 2):
        real_part, imag_part = (
            along(cos_table, real_part, axis) - along(sin_table, imag_part, axis),
            along(cos_table, imag_part, axis) + along(sin_table, real_part, axis),
        )
    result = along(cos_table, real_part, 3) - along(sin_table, imag_part, 3)
    return result / float(size**3)


def local_columns(orbitals, points, cinv):
    ranks = lax.axis_size(("grid", "col"))
    local_rows = orbitals.shape[0]
    orbital_count = orbitals.shape[1]
    npoints = cinv.shape[0]
    columns = cinv.shape[1]
    per_rank = columns // ranks
    first_row = lax.axis_index(("grid", "col")) * local_rows
    offset = points - first_row
    inside = (offset >= 0) & (offset < local_rows)
    picked = jnp.take(orbitals, jnp.clip(offset, 0, local_rows - 1), axis=0)
    picked = jnp.where(inside[:, None], picked.astype(jnp.float32), 0.0)
    point_rows = lax.psum(picked, ("grid", "col")).astype(jnp.bfloat16)
    scale = 1.0 / math.sqrt(orbital_count)
    block_rows = math.gcd(local_rows, 1152)

    def pair_block(block):
        product = (
            lax.dot_general(
                block, point_rows, (((1,), (1,)), ((), ())), preferred_element_type=jnp.float32
            )
            * scale
        )
        return (product * product).astype(jnp.bfloat16)

    pairs = lax.map(
        pair_block, orbitals.reshape(local_rows // block_rows, block_rows, orbital_count)
    )
    pairs = pairs.reshape(local_rows, npoints)
    theta_cols = lax.dot_general(
        cinv, pairs, (((0,), (1,)), ((), ())), preferred_element_type=jnp.float32
    )
    fields = lax.all_to_all(theta_cols, ("grid", "col"), split_axis=0, concat_axis=1, tiled=True)
    fields = fields.reshape(per_rank, NX, NX, NX)
    potentials = screened_solve(fields).astype(jnp.bfloat16).reshape(per_rank, NX * NX * NX)
    rows_back = lax.all_to_all(potentials, ("grid", "col"), split_axis=1, concat_axis=0, tiled=True)
    factor = math.sqrt(npoints) / float(NX**3)
    halfway = lax.psum_scatter(
        lax.dot_general(
            pairs, rows_back, (((0,), (1,)), ((), ())), preferred_element_type=jnp.float32
        )
        * factor,
        "grid",
        scatter_dimension=0,
        tiled=True,
    )
    coupling = lax.psum_scatter(halfway, "col", scatter_dimension=0, tiled=True)
    return (rows_back, coupling)


AXES = ("grid", "col")
BF16, F32 = jnp.bfloat16, jnp.float32


def basis(size):
    wave = np.arange(size)[:, None]
    cell = np.arange(size)[None, :]
    angle = 2.0 * np.pi * (wave * cell % size) / size
    rows = np.where(2 * wave <= size, np.cos(angle), np.sin(angle)) * np.sqrt(2.0 / size)
    rows[0] = np.sqrt(1.0 / size)
    if size % 2 == 0:
        rows[size // 2] *= np.sqrt(0.5)
    number = np.minimum(np.arange(size), size - np.arange(size))
    return rows, (number * (2.0 * np.pi / size)) ** 2


def split_tables(table):
    high = np.asarray(table, BF16)
    low = np.asarray(table - high.astype(np.float64), BF16)
    both = np.concatenate([high, low], axis=1)
    return jnp.asarray(both), jnp.asarray(np.concatenate([both, high], axis=1))


def dot(left, right):
    return lax.dot_general(left, right, (((1,), (0,)), ((), ())), preferred_element_type=F32)


def apply_exact(table, values):
    return dot(table, jnp.concatenate([values, values], axis=0))


def apply_split(table, values):
    high = values.astype(BF16)
    low = (values - high.astype(F32)).astype(BF16)
    return dot(table, jnp.concatenate([high, high, low], axis=0))


LANES = 128
UNROLL = 2
BLOCK = 256


def across(ref, index, size):
    rows = pl.ds(index, size, stride=size + 1)
    return jnp.concatenate([ref[half, rows, :] for half in range(ref.shape[0])], axis=1)


def put_line(ref, line, size, value):
    rows = pl.ds(line * (size + 1), size)
    for half in range(ref.shape[0]):
        ref[half, rows, :] = value[:, half * LANES : (half + 1) * LANES]


def fit_kernel(size, scale, single, orb_ref, pts_ref, cinv_ref, table_ref, *rest):
    if not single:
        rest = rest[1:]
    pair_ref, outs, (field, points, shift, theta) = rest[0], rest[1:-4], rest[-4:]
    plane, step = pl.program_id(0), pl.program_id(1)
    rows = orb_ref.shape[0]
    npoints = pts_ref.shape[0]
    thirds = outs[0].shape[1] + (0 if single else 1)
    table = table_ref[...]

    @pl.when((plane == 0) & (step == 0))
    def _():
        scaled = pts_ref[...].astype(F32) * scale
        points[...] = scaled.astype(BF16)
        square = scaled * scaled
        norm = jnp.sum(square, axis=1, keepdims=True)
        mean = norm * (jnp.sum(norm) / npoints)
        shift[...] = jnp.sum(mean * cinv_ref[...].astype(F32), axis=0, keepdims=True)

    for start in range(0, npoints, BLOCK):
        part = slice(start, start + BLOCK)
        product = lax.dot_general(
            orb_ref[...], points[part], (((1,), (1,)), ((), ())), preferred_element_type=F32
        )
        pair_ref[:, part] = (product * product).astype(BF16)
    theta[...] = dot(pair_ref[...], cinv_ref[...]) - shift[...]
    for line in range(rows // size):
        value = apply_split(table, theta[line * size : (line + 1) * size])
        put_line(field, step * (rows // size) + line, size, value)

    @pl.when(step == pl.num_programs(1) - 1)
    def _():
        def body(owner, carry):
            for third in range(thirds):
                value = across(field, owner * thirds + third, size)
                value = apply_split(table, value).astype(BF16)
                if single:
                    outs[0][owner, third] = value
                elif third < thirds - 1:
                    outs[0][owner, third, plane] = value
                else:
                    outs[1][owner, plane] = value
            return carry

        lax.fori_loop(0, size // thirds, body, 0, unroll=UNROLL)


def solve_kernel(size, start, passed, wave_b_ref, wave_c_ref, wave_a_ref, table_ref, back_ref, *rest):
    first_ref, rest_ref = rest[:2]
    most_ref, last_ref, field, solved = rest[2 + passed :]
    whole = start > 0
    owners, later = rest_ref.shape[0], rest_ref.shape[1 if whole else 2]
    wave_c = wave_c_ref[start + pl.program_id(0)]

    def widen(owner, carry):
        for plane in range(later + 1):
            if plane == 0:
                value = first_ref[owner, 0]
            else:
                value = rest_ref[owner, plane - 1] if whole else rest_ref[owner, 0, plane - 1]
            put_line(field, plane * owners + owner, size, value.astype(F32))
        return carry

    lax.fori_loop(0, owners, widen, 0)
    table, back = table_ref[...], back_ref[...]
    wave_a = wave_a_ref[...]

    def body(mode, carry):
        value = apply_exact(table, across(field, mode, size).astype(BF16))
        squared = wave_a + (wave_b_ref[mode] + wave_c)
        weight = jnp.where(squared > 0, 1.0 / (squared + screening), 0.0)
        put_line(solved, mode, size, apply_split(back, value * weight))
        return carry

    lax.fori_loop(0, size, body, 0, unroll=UNROLL)

    def narrow(owner, carry):
        for plane in range(later + 1):
            value = across(solved, plane * owners + owner, size).astype(BF16)
            if plane == later:
                last_ref[owner, 0] = value
            elif whole:
                most_ref[owner, plane] = value
            else:
                most_ref[owner, 0, plane] = value
        return carry

    lax.fori_loop(0, owners, narrow, 0)


def couple_kernel(size, first, last, factor, *rest):
    count = 1 if last else 2
    sources, (exact_ref, table_ref, pair_ref) = rest[:count], rest[count : count + 3]
    rest = rest[count + 3 :]
    if not first:
        before_ref, rest = rest[0], rest[2:]
    out_ref, total_ref, field, block, total = rest
    step = pl.program_id(0)
    table = table_ref[...]
    rows = pair_ref.shape[0]
    owners = sources[0].shape[0]
    thirds = size // owners

    @pl.when(step == 0)
    def _():
        if first:
            total[...] = jnp.zeros_like(total)
        else:
            total[...] = before_ref[...]

        def body(owner, carry):
            for third in range(thirds):
                if last:
                    value = sources[0][owner, third]
                elif third < thirds - 1:
                    value = sources[0][owner, third, 0]
                else:
                    value = sources[1][owner, 0]
                value = apply_exact(exact_ref[...], value)
                put_line(field, owner * thirds + third, size, value)
            return carry

        lax.fori_loop(0, owners, body, 0, unroll=UNROLL)

    for line in range(rows // size):
        value = across(field, step * (rows // size) + line, size)
        block[line * size : (line + 1) * size, :] = apply_split(table, value)
    turned = block[...].T.astype(BF16)
    out_ref[...] = turned
    total[...] += dot(turned, pair_ref[...])

    @pl.when(step == pl.num_programs(0) - 1)
    def _():
        if last:
            total_ref[...] = total[...].T * factor
        else:
            total_ref[...] = total[...]


def const_spec(shape):
    return pl.BlockSpec(shape, lambda *_: (0,) * len(shape))


def cost(flops, moved):
    return pl.CostEstimate(flops=int(flops), bytes_accessed=int(moved), transcendentals=0)


VMEM = 65472 * 1024


def row_blocks(size, lines):
    while size % lines:
        lines -= 1
    return lines * size, size // lines


def local_planes(orbitals, points, cinv):
    size = NX
    ranks = lax.axis_size(AXES)
    rank = lax.axis_index(AXES)
    local_rows, orbital_count = orbitals.shape
    npoints, columns = cinv.shape
    plane_rows = size * size
    planes = local_rows // plane_rows
    later = planes - 1
    halves = columns // LANES

    arrivals = []

    def exchange(array):
        if arrivals:
            array, _ = lax.optimization_barrier((array, arrivals[-1]))
        arrivals.append(lax.all_to_all(array, AXES, 0, 0, tiled=True))
        return arrivals[-1]

    chips = lax.axis_size("grid")
    core = lax.axis_index("col")

    def swap(array):
        return lax.ppermute(array, "col", [(0, 1), (1, 0)])

    def scatter_sum(array):
        array = array.reshape(chips, 2, npoints // ranks, -1)
        own = lax.dynamic_index_in_dim(array, core, 1, keepdims=False)
        array = own + swap(lax.dynamic_index_in_dim(array, 1 - core, 1, keepdims=False))
        array = lax.all_to_all(array, "grid", 0, 0, tiled=True)
        return jnp.sum(array.astype(F32), axis=0).astype(array.dtype)

    offset = points - rank * local_rows
    inside = (offset >= 0) & (offset < local_rows)
    picked = jnp.take(orbitals, jnp.clip(offset, 0, local_rows - 1), axis=0)
    picked = jnp.where(inside[:, None], picked, jnp.zeros_like(picked))
    share = scatter_sum(picked)
    share = jnp.broadcast_to(share[None], (chips, *share.shape))
    own = lax.all_to_all(share, "grid", 0, 0, tiled=True)
    both = jnp.stack([own, swap(own)], axis=1)
    point_rows = jnp.where(core == 0, both, both[:, ::-1]).reshape(npoints, orbital_count)

    rows, squared = basis(size)
    _, forward = split_tables(rows)
    inverse_exact, inverse = split_tables(rows.T)
    order = (np.arange(ranks)[None, :] * planes + np.arange(planes)[:, None]).reshape(-1)
    forward_a, _ = split_tables(rows[:, order])
    _, inverse_a = split_tables(rows.T[order])
    wave = jnp.asarray(squared, F32)
    wave_a = jnp.asarray(np.broadcast_to(squared[:, None], (size, columns)), F32)

    block_rows, steps = row_blocks(size, 16)
    scale = 1.0 / math.sqrt(orbital_count)
    transform = 2 * 3 * plane_rows * size * columns
    tile = (size, columns)

    smem = pl.BlockSpec(memory_space=pltpu.SMEM)
    anywhere = pl.BlockSpec(memory_space=pl.ANY)

    def fit(start, count, *after):
        if count == 1 and start == 0:
            shapes = [(ranks, planes, *tile)]
        else:
            shapes = [(ranks, planes - 1, count, *tile), (ranks, count, *tile)]
        pair, *sent = pl.pallas_call(
            functools.partial(fit_kernel, size, scale, start == 0),
            grid=(count, steps),
            in_specs=[
                pl.BlockSpec((block_rows, orbital_count), lambda p, i: ((start + p) * steps + i, 0)),
                const_spec((npoints, orbital_count)),
                const_spec((npoints, columns)),
                const_spec(forward.shape),
            ]
            + [anywhere] * len(after),
            out_specs=[pl.BlockSpec((block_rows, npoints), lambda p, i: (p * steps + i, 0))]
            + [const_spec(shape) for shape in shapes],
            out_shape=[jax.ShapeDtypeStruct((count * plane_rows, npoints), BF16)]
            + [jax.ShapeDtypeStruct(shape, BF16) for shape in shapes],
            scratch_shapes=[
                pltpu.VMEM((halves, size * (size + 1), LANES), F32),
                pltpu.VMEM((npoints, orbital_count), BF16),
                pltpu.VMEM((1, columns), F32),
                pltpu.VMEM((block_rows, columns), F32),
            ],
            compiler_params=pltpu.CompilerParams(
                dimension_semantics=("arbitrary", "arbitrary"), vmem_limit_bytes=VMEM
            ),
            cost_estimate=cost(
                count * (2 * plane_rows * npoints * (orbital_count + columns) + 2 * transform),
                count * plane_rows * (2 * orbital_count + 2 * npoints + 2 * columns),
            ),
            name="fit",
        )(orbitals, point_rows, cinv, forward, *after)
        return pair, sent

    pair_first, (sent_first,) = fit(0, 1)
    arrived_first = exchange(sent_first)
    pair_rest, sent_rest = fit(1, later, pair_first)
    arrived_most, arrived_last = [exchange(value) for value in sent_rest]

    wave_c = lax.dynamic_slice(wave, (rank * planes,), (planes,))

    def solve(start, count, arrived, *passed):
        operands = [wave, wave_c, wave_a, forward_a, inverse_a, arrived_first, arrived, *passed]
        third_spec = pl.BlockSpec((ranks, 1, *tile), lambda i: (0, start + i, 0, 0))
        if start > 0:
            most_shape = (ranks, later, *tile)
            most_spec = const_spec(most_shape)
        else:
            most_shape = (ranks, count, later, *tile)
            most_spec = pl.BlockSpec((ranks, 1, later, *tile), lambda i: (0, i, 0, 0, 0))
        return pl.pallas_call(
            functools.partial(solve_kernel, size, start, len(passed)),
            grid=(count,),
            in_specs=[smem, smem]
            + [const_spec(value.shape) for value in operands[2:5]]
            + [third_spec, most_spec]
            + [anywhere] * len(passed),
            out_specs=[most_spec, third_spec],
            out_shape=[
                jax.ShapeDtypeStruct(most_shape, BF16),
                jax.ShapeDtypeStruct((ranks, planes, *tile), BF16),
            ],
            scratch_shapes=[pltpu.VMEM((halves, size * (size + 1), LANES), F32)] * 2,
            input_output_aliases={7: 1} if passed else {},
            compiler_params=pltpu.CompilerParams(
                dimension_semantics=("arbitrary",), vmem_limit_bytes=VMEM
            ),
            cost_estimate=cost(2 * count * transform, 4 * count * plane_rows * columns),
            name="solve",
        )(*operands)

    back_most, back_end = solve(0, later, arrived_most)
    arrived_most = exchange(back_most)
    back_last, back_end = solve(later, 1, arrived_last, back_end)
    arrived_last = exchange(back_last)
    arrived_end = exchange(back_end)

    factor = math.sqrt(npoints) / float(size**3)
    block_rows, steps = row_blocks(size, 8)
    potential = total = None
    for plane in range(planes):
        first, last = plane == 0, plane == planes - 1
        pair_start = 0 if first else (plane - 1) * steps
        if last:
            sources, in_specs = [arrived_end], [const_spec(arrived_end.shape)]
        else:
            sources = [arrived_most, arrived_last]
            in_specs = [
                pl.BlockSpec((ranks, later, 1, *tile), lambda i, plane=plane: (0, 0, plane, 0, 0)),
                pl.BlockSpec((ranks, 1, *tile), lambda i, plane=plane: (0, plane, 0, 0)),
            ]
        in_specs += [
            const_spec(inverse_exact.shape),
            const_spec(inverse.shape),
            pl.BlockSpec((block_rows, npoints), lambda i, start=pair_start: (start + i, 0)),
        ]
        operands = [*sources, inverse_exact, inverse, pair_first if first else pair_rest]
        if not first:
            in_specs += [const_spec(total.shape), anywhere]
            operands += [total, potential]
        total_shape = (npoints, columns) if last else (columns, npoints)
        potential, total = pl.pallas_call(
            functools.partial(couple_kernel, size, first, last, factor),
            grid=(steps,),
            in_specs=in_specs,
            out_specs=[
                pl.BlockSpec((columns, block_rows), lambda i, plane=plane: (0, plane * steps + i)),
                const_spec(total_shape),
            ],
            out_shape=[
                jax.ShapeDtypeStruct((columns, local_rows), BF16),
                jax.ShapeDtypeStruct(total_shape, F32),
            ],
            scratch_shapes=[
                pltpu.VMEM((halves, size * (size + 1), LANES), F32),
                pltpu.VMEM((block_rows, columns), F32),
                pltpu.VMEM((columns, npoints), F32),
            ],
            input_output_aliases={} if first else {len(operands) - 1: 0},
            compiler_params=pltpu.CompilerParams(
                dimension_semantics=("arbitrary",), vmem_limit_bytes=VMEM
            ),
            cost_estimate=cost(
                2 * plane_rows * npoints * columns + 2 * transform,
                plane_rows * (2 * npoints + 4 * columns),
            ),
            name="couple",
        )(*operands)

    return potential, scatter_sum(total)


def local(orbitals, points, cinv):
    size = NX
    ranks = lax.axis_size(AXES)
    rows, orbital_count = orbitals.shape
    npoints, columns = cinv.shape
    whole = rows * ranks == size**3 and rows % (size * size) == 0 and size % 16 == 0
    whole = whole and rows >= 2 * size * size and lax.axis_size("col") == 2
    exact = math.frexp(1.0 / math.sqrt(orbital_count))[0] == 0.5
    if whole and exact and columns % LANES == 0 and npoints % (ranks * 8) == 0:
        return local_planes(orbitals, points, cinv)
    return local_columns(orbitals, points, cinv)


def solution(mesh):
    in_specs = (P(("grid", "col"), None), P(), P())
    out_specs = (P(None, ("grid", "col")), P(("grid", "col"), None))
    return jax.shard_map(local, mesh=mesh, in_specs=in_specs, out_specs=out_specs, check_vma=False)
```

profile of v0, /device:TPU:0, one launch (start us, length us, event | category | flops | bytes accessed | tf_op | source)
XLA Modules:
  0.0 779.2 jit_solution(4491540077249734945)
XLA Ops:
  0.6 0.7 compare_and_fusion.1
  1.3 0.7 fusion
  2.0 0.1 broadcast_in_dim.34
  2.1 0.1 broadcast_in_dim.36
  2.2 10.3 %gather_fusion = bf16[1024,256]{1,0:T(8,128)(2,1)S(1)} fusion(bf16[27648,256]{1,0:T(8,128)(2,1)} %orb_ref.3, s32[1024]{0:T(1024)S(1)} %fusion), kind=kCustom, calls=%fused_computation | custom fusion | bytes 1052672 | tf_op jit(solution)/shard_map/jit(_take)/gather | solution.py:351
  12.5 0.3 select_select_fusion
  12.9 0.6 collective-permute-start
  13.4 1.2 collective-permute-done
  14.6 18.2 %all_to_all.45 = bf16[16,32,256]{2,1,0:T(8,128)(2,1)S(1)} all-to-all(bf16[16,32,256]{2,1,0:T(8,128)(2,1)S(1)} %bitcast_add_fusion.1), channel_id=1, replica_groups=mesh['grid'=16,'col'=2] {'grid'}, dimensions={0} | all-to-all | bytes 524288 | tf_op jit(solution)/shard_map/all_to_all | solution.py:346
  32.9 12.8 %all_to_all.46 = bf16[16,32,256]{2,1,0:T(8,128)(2,1)S(1)} all-to-all(bf16[16,32,256]{2,1,0:T(8,128)(2,1)S(1)} %broadcast_in_dim.41), channel_id=1, replica_groups=mesh['grid'=16,'col'=2] {'grid'}, dimensions={0} | all-to-all | bytes 524288 | tf_op jit(solution)/shard_map/all_to_all | solution.py:355
  45.7 0.0 collective-permute-start.1
  45.7 1.5 collective-permute-done.1
  47.2 0.1 pad_maximum_fusion
  47.3 0.9 reverse_select_fusion
  48.2 29.0 %fit.2 = (bf16[9216,1024]{1,0:T(8,128)(2,1)}, bf16[32,3,96,256]{3,2,1,0:T(8,128)(2,1)}) custom-call(bf16[27648,256]{1,0:T(8,128)(2,1)} %orb_ref.3, bf16[1024,256]{1,0:T(8,128)(2,1)} %bitcast.19, bf16[1024,256]{1,0:T(8,128)(2,1)} %cinv_ref.3, bf16[96,288]{1,0:T(8,128)(2,1)} %constant.69.clone.table_ref), custom_call_target="tpu_custom_call" | custom-call | flops 12381585408 | bytes 28311552 | tf_op jit(solution)/shard_map/fit/pallas_call | solution.py:381
  77.2 3.6 all-to-all-start.2
  80.8 54.7 %fit.3 = (bf16[18432,1024]{1,0:T(8,128)(2,1)}, bf16[32,2,2,96,256]{4,3,2,1,0:T(8,128)(2,1)}, bf16[32,2,96,256]{3,2,1,0:T(8,128)(2,1)}) custom-call(bf16[27648,256]{1,0:T(8,128)(2,1)} %orb_ref.3, bf16[1024,256]{1,0:T(8,128)(2,1)} %bitcast.20, bf16[1024,256]{1,0:T(8,128)(2,1)} %cinv_ref.3, bf16[96,288]{1,0:T(8,128)(2,1)} %constant.69.clone.table_ref, ...), custom_call_target="tpu_custom_call" | custom-call | flops 24763170816 | bytes 56623104 | tf_op jit(solution)/shard_map/fit/pallas_call | solution.py:381
  135.6 50.4 %all-to-all-done.2.rest_0_ = bf16[32,3,96,256]{3,2,1,0:T(8,128)(2,1)} async-done(((bf16[32,3,96,256]{3,2,1,0:T(8,128)(2,1)}), bf16[32,3,96,256]{3,2,1,0:T(8,128)(2,1)}, u32[]{:S(2)}, u32[]{:S(2)}) %all-to-all-start.2) | async-done | bytes 4718624 | tf_op jit(solution)/shard_map/all_to_all | solution.py:333
  186.0 142.5 %all_to_all.47.rest_1_ = bf16[32,2,2,96,256]{4,3,2,1,0:T(8,128)(2,1)} all-to-all(bf16[32,2,2,96,256]{4,3,2,1,0:T(8,128)(2,1)} %get-tuple-element.26), channel_id=1, replica_groups=mesh['grid'=16,'col'=2] {'grid','col'}, dimensions={0} | all-to-all | bytes 12582912 | tf_op jit(solution)/shard_map/all_to_all | solution.py:333
  328.5 0.0 copy-start
  328.5 3.8 all-to-all-start.4
  332.3 0.0 copy-done
  332.3 0.6 dynamic_slice.17.wave_c_ref
  332.9 44.1 %solve.2 = (bf16[32,2,2,96,256]{4,3,2,1,0:T(8,128)(2,1)}, bf16[32,3,96,256]{3,2,1,0:T(8,128)(2,1)}) custom-call(f32[96]{0:T(128)} %constant.74.clone.wave_b_ref, f32[3]{0:T(128)} %dynamic_slice.17.wave_c_ref, f32[96,256]{1,0:T(8,128)} %constant.75.clone.wave_a_ref, bf16[96,192]{1,0:T(8,128)(2,1)} %constant.72.clone.table_ref, ...), custom_call_target="tpu_custom_call" | custom-call | flops 5435817984 | bytes 18874368 | tf_op jit(solution)/shard_map/solve/pallas_call | solution.py:428
  377.1 26.6 %all-to-all-done.4.rest_1_ = bf16[32,2,96,256]{3,2,1,0:T(8,128)(2,1)} async-done(((bf16[32,2,96,256]{3,2,1,0:T(8,128)(2,1)}), bf16[32,2,96,256]{3,2,1,0:T(8,128)(2,1)}, u32[]{:S(2)}, u32[]{:S(2)}) %all-to-all-start.4) | async-done | bytes 3145760 | tf_op jit(solution)/shard_map/all_to_all | solution.py:333
  403.7 4.1 all-to-all-start.5
  407.8 24.4 %solve.3 = (bf16[32,2,96,256]{3,2,1,0:T(8,128)(2,1)}, bf16[32,3,96,256]{3,2,1,0:T(8,128)(2,1)}) custom-call(f32[96]{0:T(128)} %constant.74.clone.wave_b_ref, f32[3]{0:T(128)} %dynamic_slice.17.wave_c_ref, f32[96,256]{1,0:T(8,128)} %constant.75.clone.wave_a_ref, bf16[96,192]{1,0:T(8,128)(2,1)} %constant.72.clone.table_ref, ...), custom_call_target="tpu_custom_call", output_to_operand_aliasing={{1}: (7, {})} | custom-call | flops 2717908992 | bytes 9437184 | tf_op jit(solution)/shard_map/solve/pallas_call | solution.py:428
  432.2 115.4 %all-to-all-done.5.rest_0_ = bf16[32,2,2,96,256]{4,3,2,1,0:T(8,128)(2,1)} async-done(((bf16[32,2,2,96,256]{4,3,2,1,0:T(8,128)(2,1)}), bf16[32,2,2,96,256]{4,3,2,1,0:T(8,128)(2,1)}, u32[]{:S(2)}, u32[]{:S(2)}) %all-to-all-start.5) | async-done | bytes 6291488 | tf_op jit(solution)/shard_map/all_to_all | solution.py:333
  547.6 74.7 %all_to_all.48.rest_1_ = bf16[32,2,96,256]{3,2,1,0:T(8,128)(2,1)} all-to-all(bf16[32,2,96,256]{3,2,1,0:T(8,128)(2,1)} %get-tuple-element.33), channel_id=1, replica_groups=mesh['grid'=16,'col'=2] {'grid','col'}, dimensions={0} | all-to-all | bytes 6291456 | tf_op jit(solution)/shard_map/all_to_all | solution.py:333
  622.2 3.8 all-to-all-start.7
  626.0 22.8 %couple.3 = (bf16[256,27648]{1,0:T(8,128)(2,1)}, f32[256,1024]{1,0:T(8,128)}) custom-call(bf16[32,2,2,96,256]{4,3,2,1,0:T(8,128)(2,1)} %all-to-all-done.5.rest_0_, bf16[32,2,96,256]{3,2,1,0:T(8,128)(2,1)} %all_to_all.48.rest_1_, bf16[96,192]{1,0:T(8,128)(2,1)} %constant.70.clone.rest_2_.rest_1_, bf16[96,288]{1,0:T(8,128)(2,1)} %constant.71.clone.rest_3_.rest_2_, ...), custom_call_target="tpu_custom_call" | custom-call | flops 7549747200 | bytes 28311552 | tf_op jit(solution)/shard_map/couple/pallas_call | solution.py:479
  648.8 23.0 %couple.4 = (bf16[256,27648]{1,0:T(8,128)(2,1)}, f32[256,1024]{1,0:T(8,128)}) custom-call(bf16[32,2,2,96,256]{4,3,2,1,0:T(8,128)(2,1)} %all-to-all-done.5.rest_0_, bf16[32,2,96,256]{3,2,1,0:T(8,128)(2,1)} %all_to_all.48.rest_1_, bf16[96,192]{1,0:T(8,128)(2,1)} %constant.70.clone.rest_2_.rest_1_, ...), custom_call_target="tpu_custom_call", output_to_operand_aliasing={{0}: (6, {})} | custom-call | flops 7549747200 | bytes 28311552 | tf_op jit(solution)/shard_map/couple/pallas_call | solution.py:479
  671.8 59.2 %all-to-all-done.7.rest_0_ = bf16[32,3,96,256]{3,2,1,0:T(8,128)(2,1)} async-done(((bf16[32,3,96,256]{3,2,1,0:T(8,128)(2,1)}), bf16[32,3,96,256]{3,2,1,0:T(8,128)(2,1)}, u32[]{:S(2)}, u32[]{:S(2)}) %all-to-all-start.7) | async-done | bytes 4718624 | tf_op jit(solution)/shard_map/all_to_all | solution.py:333
  731.0 23.2 %couple.5 = (bf16[256,27648]{1,0:T(8,128)(2,1)}, f32[1024,256]{1,0:T(8,128)}) custom-call(bf16[32,3,96,256]{3,2,1,0:T(8,128)(2,1)} %all-to-all-done.7.rest_0_, bf16[96,192]{1,0:T(8,128)(2,1)} %constant.70.clone.rest_2_.rest_1_, bf16[96,288]{1,0:T(8,128)(2,1)} %constant.71.clone.rest_3_.rest_2_, ...), custom_call_target="tpu_custom_call", output_to_operand_aliasing={{0}: (5, {})} | custom-call | flops 7549747200 | bytes 28311552 | tf_op jit(solution)/shard_map/couple/pallas_call | solution.py:479
  754.3 1.1 dynamic-slice_bitcast_fusion
  755.3 0.1 collective-permute-start.2
  755.4 1.9 collective-permute-done.2
  757.3 1.1 bitcast_add_fusion
  758.4 20.1 %all_to_all.49 = f32[16,32,256]{2,1,0:T(8,128)S(1)} all-to-all(f32[16,32,256]{2,1,0:T(8,128)S(1)} %bitcast_add_fusion), channel_id=1, replica_groups=mesh['grid'=16,'col'=2] {'grid'}, dimensions={0} | all-to-all | bytes 1048576 | tf_op jit(solution)/shard_map/all_to_all | solution.py:346
  778.6 0.6 reduce_sum.22
  (4 shorter events, 0.1 us)
Async XLA Ops:
  12.9 1.7 collective-permute-start
  45.7 1.5 collective-permute-start.1
  77.2 108.7 %all-to-all-start.2 = ((bf16[32,3,96,256]{3,2,1,0:T(8,128)(2,1)}), bf16[32,3,96,256]{3,2,1,0:T(8,128)(2,1)}, u32[]{:S(2)}, u32[]{:S(2)}) async-start(bf16[32,3,96,256]{3,2,1,0:T(8,128)(2,1)} %get-tuple-element.22), calls=%async_computation.2 | async-start | bytes 9437184 | tf_op jit(solution)/shard_map/all_to_all | solution.py:333
  328.5 3.8 copy-start
  328.5 75.2 %all-to-all-start.4 = ((bf16[32,2,96,256]{3,2,1,0:T(8,128)(2,1)}), bf16[32,2,96,256]{3,2,1,0:T(8,128)(2,1)}, u32[]{:S(2)}, u32[]{:S(2)}) async-start(bf16[32,2,96,256]{3,2,1,0:T(8,128)(2,1)} %get-tuple-element.27), calls=%async_computation.4 | async-start | bytes 6291456 | tf_op jit(solution)/shard_map/all_to_all | solution.py:333
  403.7 143.9 %all-to-all-start.5 = ((bf16[32,2,2,96,256]{4,3,2,1,0:T(8,128)(2,1)}), bf16[32,2,2,96,256]{4,3,2,1,0:T(8,128)(2,1)}, u32[]{:S(2)}, u32[]{:S(2)}) async-start(bf16[32,2,2,96,256]{4,3,2,1,0:T(8,128)(2,1)} %get-tuple-element.32), calls=%async_computation.5 | async-start | bytes 12582912 | tf_op jit(solution)/shard_map/all_to_all | solution.py:333
  622.2 108.8 %all-to-all-start.7 = ((bf16[32,3,96,256]{3,2,1,0:T(8,128)(2,1)}), bf16[32,3,96,256]{3,2,1,0:T(8,128)(2,1)}, u32[]{:S(2)}, u32[]{:S(2)}) async-start(bf16[32,3,96,256]{3,2,1,0:T(8,128)(2,1)} %get-tuple-element.34), calls=%async_computation.7 | async-start | bytes 9437184 | tf_op jit(solution)/shard_map/all_to_all | solution.py:333
  755.3 2.0 collective-permute-start.2
where the time goes:
time: 781 us; the launch traced here: 779 us
  blocking collectives  268 us (34%)
  waiting for transfers between devices  256 us (33%)
  Pallas kernels  221 us (28%)
  starting transfers between devices  15.9 us (2%)
  local copies, waits for them, and re-layouts  12.2 us (2%)
    all_to_all x4, waiting for transfers between devices, exchange(): arrivals.append(lax.all_to_all(array, AXES, 0, 0, tiled=True))  252 us
    all_to_all x2, blocking collectives, exchange(): arrivals.append(lax.all_to_all(array, AXES, 0, 0, tiled=True))  217 us
    pallas_call x2, Pallas kernels, fit(): pl.pallas_call(functools.partial(fit_kernel, size, scale, start == 0), gr...  83.8 us
    pallas_call x3, Pallas kernels, local_planes(): pl.pallas_call(functools.partial(couple_kernel, size, first, last, factor...  69.1 us
    pallas_call x2, Pallas kernels, solve(): pl.pallas_call(functools.partial(solve_kernel, size, start, len(passed)),...  68.5 us
    all_to_all x2, blocking collectives, scatter_sum(): array = lax.all_to_all(array, 'grid', 0, 0, tiled=True)  38.3 us
  transfers between devices with their start and end apart: 7, of which 7 were waited for; matrix products, arithmetic and copies ran while one was open for 0% of the time, Pallas kernels for 22%

commit v1 on v0

--- a/solution.py
+++ b/solution.py
@@ -8,6 +8,7 @@
 from jax.experimental import pallas as pl
 from jax.experimental.pallas import tpu as pltpu
 from jax.sharding import PartitionSpec as P
+
 
 NX = 96
 
@@ -248,16 +249,18 @@
     lax.fori_loop(0, owners, narrow, 0)
 
 
-def couple_kernel(size, first, last, factor, *rest):
+def couple_kernel(size, first, last, rows, *rest):
     count = 1 if last else 2
     sources, (exact_ref, table_ref, pair_ref) = rest[:count], rest[count : count + 3]
     rest = rest[count + 3 :]
-    if not first:
-        before_ref, rest = rest[0], rest[2:]
-    out_ref, total_ref, field, block, total = rest
+    if last:
+        out_ref, field, block = rest[2:]
+    else:
+        if not first:
+            before_ref, rest = rest[0], rest[2:]
+        out_ref, total_ref, field, block, total = rest
     step = pl.program_id(0)
     table = table_ref[...]
-    rows = pair_ref.shape[0]
     owners = sources[0].shape[0]
     thirds = size // owners
 
@@ -265,7 +268,7 @@
     def _():
         if first:
             total[...] = jnp.zeros_like(total)
-        else:
+        elif not last:
             total[...] = before_ref[...]
 
         def body(owner, carry):
@@ -287,14 +290,54 @@
         block[line * size : (line + 1) * size, :] = apply_split(table, value)
     turned = block[...].T.astype(BF16)
     out_ref[...] = turned
+    if last:
+        return
     total[...] += dot(turned, pair_ref[...])
 
     @pl.when(step == pl.num_programs(0) - 1)
     def _():
-        if last:
-            total_ref[...] = total[...].T * factor
-        else:
-            total_ref[...] = total[...]
+        total_ref[...] = total[...]
+
+
+def spectrum_kernel(size, exact_ref, table_ref, pair_ref, out_ref, low_ref, field, block):
+    step = pl.program_id(1)
+    rows = pair_ref.shape[0]
+    lines = block.shape[0] // size
+    for line in range(rows // size):
+        value = apply_exact(exact_ref[...], pair_ref[line * size : (line + 1) * size, :])
+        put_line(field, step * (rows // size) + line, size, value)
+
+    @pl.when(step == pl.num_programs(1) - 1)
+    def _():
+        value = apply_split(table_ref[...], across(field, 0, size))
+        low_ref[...] = (value - value.astype(BF16).astype(F32)).astype(BF16)
+
+        def body(group, carry):
+            for line in range(lines):
+                value = apply_split(table_ref[...], across(field, group * lines + line, size))
+                block[line * size : (line + 1) * size, :] = value.astype(BF16)
+            start = pl.multiple_of(group * lines * size, lines * size)
+            out_ref[:, pl.ds(start, lines * size)] = block[...].T
+            return carry
+
+        lax.fori_loop(0, size // lines, body, 0)
+
+
+def contract_kernel(size, factor, before_ref, low_ref, left_ref, right_ref, out_ref):
+    step = pl.program_id(0)
+
+    @pl.when(step == 0)
+    def _():
+        low = lax.dot_general(
+            low_ref[...], right_ref[:size, :], (((0,), (0,)), ((), ())), preferred_element_type=F32
+        )
+        out_ref[...] = before_ref[...].T + low
+
+    out_ref[...] += dot(left_ref[...], right_ref[...])
+
+    @pl.when(step == pl.num_programs(0) - 1)
+    def _():
+        out_ref[...] = out_ref[...] * factor
 
 
 def const_spec(shape):
@@ -339,25 +382,24 @@
     def swap(array):
         return lax.ppermute(array, "col", [(0, 1), (1, 0)])
 
-    def scatter_sum(array):
+    def pair_sum(array):
         array = array.reshape(chips, 2, npoints // ranks, -1)
         own = lax.dynamic_index_in_dim(array, core, 1, keepdims=False)
-        array = own + swap(lax.dynamic_index_in_dim(array, 1 - core, 1, keepdims=False))
-        array = lax.all_to_all(array, "grid", 0, 0, tiled=True)
-        return jnp.sum(array.astype(F32), axis=0).astype(array.dtype)
+        return own + swap(lax.dynamic_index_in_dim(array, 1 - core, 1, keepdims=False))
 
     offset = points - rank * local_rows
     inside = (offset >= 0) & (offset < local_rows)
     picked = jnp.take(orbitals, jnp.clip(offset, 0, local_rows - 1), axis=0)
     picked = jnp.where(inside[:, None], picked, jnp.zeros_like(picked))
-    share = scatter_sum(picked)
+    shares = lax.all_to_all(pair_sum(picked), "grid", 0, 0, tiled=True)
+    share = jnp.sum(shares.astype(F32), axis=0).astype(BF16)
     share = jnp.broadcast_to(share[None], (chips, *share.shape))
     own = lax.all_to_all(share, "grid", 0, 0, tiled=True)
     both = jnp.stack([own, swap(own)], axis=1)
     point_rows = jnp.where(core == 0, both, both[:, ::-1]).reshape(npoints, orbital_count)
 
     rows, squared = basis(size)
-    _, forward = split_tables(rows)
+    forward_exact, forward = split_tables(rows)
     inverse_exact, inverse = split_tables(rows.T)
     order = (np.arange(ranks)[None, :] * planes + np.arange(planes)[:, None]).reshape(-1)
     forward_a, _ = split_tables(rows[:, order])
@@ -449,11 +491,40 @@
     back_most, back_end = solve(0, later, arrived_most)
     arrived_most = exchange(back_most)
     back_last, back_end = solve(later, 1, arrived_last, back_end)
+    block_rows, steps = row_blocks(size, 8)
+    params = pltpu.CompilerParams(dimension_semantics=("arbitrary",), vmem_limit_bytes=VMEM)
+    field = pltpu.VMEM((halves, size * (size + 1), LANES), F32)
+    last_start = (later - 1) * steps
+    modes, low = pl.pallas_call(
+        functools.partial(spectrum_kernel, size),
+        grid=(npoints // columns, steps),
+        in_specs=[
+            const_spec(forward_exact.shape),
+            const_spec(forward.shape),
+            pl.BlockSpec((block_rows, columns), lambda g, i: (last_start + i, g)),
+        ],
+        out_specs=[
+            pl.BlockSpec((columns, plane_rows), lambda g, i: (g, 0)),
+            pl.BlockSpec((size, columns), lambda g, i: (0, g)),
+        ],
+        out_shape=[
+            jax.ShapeDtypeStruct((npoints, plane_rows), BF16),
+            jax.ShapeDtypeStruct((size, npoints), BF16),
+        ],
+        scratch_shapes=[field, pltpu.VMEM((4 * size, columns), BF16)],
+        compiler_params=pltpu.CompilerParams(
+            dimension_semantics=("arbitrary", "arbitrary"), vmem_limit_bytes=VMEM
+        ),
+        cost_estimate=cost(
+            2 * transform * npoints // columns, 4 * plane_rows * npoints
+        ),
+        name="spectrum",
+    )(forward_exact, forward, pair_rest)
+    back_last, modes, low = lax.optimization_barrier((back_last, modes, low))
     arrived_last = exchange(back_last)
     arrived_end = exchange(back_end)
 
     factor = math.sqrt(npoints) / float(size**3)
-    block_rows, steps = row_blocks(size, 8)
     potential = total = None
     for plane in range(planes):
         first, last = plane == 0, plane == planes - 1
@@ -472,39 +543,64 @@
             pl.BlockSpec((block_rows, npoints), lambda i, start=pair_start: (start + i, 0)),
         ]
         operands = [*sources, inverse_exact, inverse, pair_first if first else pair_rest]
-        if not first:
+        if last:
+            total = pl.pallas_call(
+                functools.partial(contract_kernel, size, factor),
+                grid=(steps,),
+                in_specs=[
+                    const_spec(total.shape),
+                    const_spec(low.shape),
+                    pl.BlockSpec((npoints, block_rows), lambda i: (0, i)),
+                    pl.BlockSpec((block_rows, columns), lambda i: (i, 0)),
+                ],
+                out_specs=const_spec((npoints, columns)),
+                out_shape=jax.ShapeDtypeStruct((npoints, columns), F32),
+                compiler_params=params,
+                cost_estimate=cost(
+                    2 * plane_rows * npoints * columns, 2 * plane_rows * (npoints + columns)
+                ),
+                name="contract",
+            )(total, low, modes, arrived_end.reshape(plane_rows, columns))
+            total = pair_sum(total)
+            operands[-1] = jnp.zeros((16, LANES), BF16)
+            in_specs[-1] = const_spec((16, LANES))
+            in_specs += [anywhere, anywhere]
+            operands += [total, potential]
+        elif not first:
             in_specs += [const_spec(total.shape), anywhere]
             operands += [total, potential]
-        total_shape = (npoints, columns) if last else (columns, npoints)
-        potential, total = pl.pallas_call(
-            functools.partial(couple_kernel, size, first, last, factor),
+        call = pl.pallas_call(
+            functools.partial(couple_kernel, size, first, last, block_rows),
             grid=(steps,),
             in_specs=in_specs,
             out_specs=[
                 pl.BlockSpec((columns, block_rows), lambda i, plane=plane: (0, plane * steps + i)),
-                const_spec(total_shape),
-            ],
+                const_spec((columns, npoints)),
+            ][: 1 if last else 2],
             out_shape=[
                 jax.ShapeDtypeStruct((columns, local_rows), BF16),
-                jax.ShapeDtypeStruct(total_shape, F32),
-            ],
+                jax.ShapeDtypeStruct((columns, npoints), F32),
+            ][: 1 if last else 2],
             scratch_shapes=[
-                pltpu.VMEM((halves, size * (size + 1), LANES), F32),
+                field,
                 pltpu.VMEM((block_rows, columns), F32),
                 pltpu.VMEM((columns, npoints), F32),
-            ],
+            ][: 2 if last else 3],
             input_output_aliases={} if first else {len(operands) - 1: 0},
-            compiler_params=pltpu.CompilerParams(
-                dimension_semantics=("arbitrary",), vmem_limit_bytes=VMEM
-            ),
+            compiler_params=params,
             cost_estimate=cost(
                 2 * plane_rows * npoints * columns + 2 * transform,
                 plane_rows * (2 * npoints + 4 * columns),
             ),
             name="couple",
-        )(*operands)
-
-    return potential, scatter_sum(total)
+        )
+        if last:
+            (potential,) = call(*operands)
+        else:
+            potential, total = call(*operands)
+
+    shares = lax.all_to_all(total, "grid", 0, 0, tiled=True)
+    return potential, jnp.sum(shares, axis=0)
 
 
 def local(orbitals, points, cinv):
@@ -523,4 +619,6 @@
 def solution(mesh):
     in_specs = (P(("grid", "col"), None), P(), P())
     out_specs = (P(None, ("grid", "col")), P(("grid", "col"), None))
-    return jax.shard_map(local, mesh=mesh, in_specs=in_specs, out_specs=out_specs, check_vma=False)
+    return jax.shard_map(
+        local, mesh=mesh, in_specs=in_specs, out_specs=out_specs, check_vma=False
+    )

time: 781 us -> 776 us (level)
  Pallas kernels: 221 us -> 300 us
  waiting for transfers between devices: 256 us -> 184 us
  blocking collectives: 268 us -> 248 us
    pallas_call x3 -> x5, Pallas kernels: 69.1 us -> 148 us  [the longest x1 72.2 us: local_planes(): pl.pallas_call(functools.partial(spectrum_kernel, size), grid=(npoints //...]
    all_to_all x4, waiting for transfers between devices: 252 us -> 179 us  [exchange(): arrivals.append(lax.all_to_all(array, AXES, 0, 0, tiled=True))]
    all_to_all x2 -> x1, blocking collectives: 38.3 us -> 18.2 us  [local_planes(): shares = lax.all_to_all(pair_sum(picked), 'grid', 0, 0, tiled=True)]
  transfers between devices with their start and end apart: 7 -> 8, of which waited for: 7 -> 8; matrix products, arithmetic and copies ran while one was open for 0% -> 0% of each run, Pallas kernels for 22% -> 33%
where the time goes in v1:
time: 776 us; the launch traced here: 774 us
  Pallas kernels  300 us (39%)
  blocking collectives  248 us (32%)
  waiting for transfers between devices  184 us (24%)
  starting transfers between devices  21.1 us (3%)
  local copies, waits for them, and re-layouts  12.8 us (2%)
    all_to_all x2, blocking collectives, exchange(): arrivals.append(lax.all_to_all(array, AXES, 0, 0, tiled=True))  217 us
    all_to_all x4, waiting for transfers between devices, exchange(): arrivals.append(lax.all_to_all(array, AXES, 0, 0, tiled=True))  179 us
    pallas_call x2, Pallas kernels, fit(): pl.pallas_call(functools.partial(fit_kernel, size, scale, start == 0), gr...  83.7 us
    pallas_call x1, Pallas kernels, local_planes(): pl.pallas_call(functools.partial(spectrum_kernel, size), grid=(npoints //...  72.2 us
    pallas_call x2, Pallas kernels, solve(): pl.pallas_call(functools.partial(solve_kernel, size, start, len(passed)),...  68.6 us
    pallas_call x2, Pallas kernels, local_planes(): potential, total = call(*operands)  45.8 us
    all_to_all x1, blocking collectives, local_planes(): shares = lax.all_to_all(pair_sum(picked), 'grid', 0, 0, tiled=True)  18.2 us
    pallas_call x1, Pallas kernels, local_planes(): pl.pallas_call(functools.partial(contract_kernel, size, factor), grid=(st...  15.7 us
  transfers between devices with their start and end apart: 8, of which 8 were waited for; matrix products, arithmetic and copies ran while one was open for 0% of the time, Pallas kernels for 33%

profile of v1, /device:TPU:0, one launch (start us, length us, event | category | flops | bytes accessed | tf_op | source)
XLA Modules:
  0.0 773.9 jit_solution(1771922863663385736)
XLA Ops:
  0.6 0.7 compare_and_fusion.1
  1.3 0.7 fusion
  2.0 0.1 broadcast_in_dim.37
  2.1 0.1 broadcast_in_dim.39
  2.2 10.3 %gather_fusion = bf16[1024,256]{1,0:T(8,128)(2,1)S(1)} fusion(bf16[27648,256]{1,0:T(8,128)(2,1)} %orb_ref.3, s32[1024]{0:T(1024)S(1)} %fusion), kind=kCustom, calls=%fused_computation | custom fusion | bytes 1052672 | tf_op jit(solution)/shard_map/jit(_take)/gather | solution.py:392
  12.5 0.3 select_select_fusion
  12.9 0.6 collective-permute-start
  13.4 1.2 collective-permute-done
  14.6 18.2 %all_to_all.45 = bf16[16,32,256]{2,1,0:T(8,128)(2,1)S(1)} all-to-all(bf16[16,32,256]{2,1,0:T(8,128)(2,1)S(1)} %bitcast_add_fusion.1), channel_id=1, replica_groups=mesh['grid'=16,'col'=2] {'grid'}, dimensions={0} | all-to-all | bytes 524288 | tf_op jit(solution)/shard_map/all_to_all | solution.py:394
  32.9 12.8 %all_to_all.46 = bf16[16,32,256]{2,1,0:T(8,128)(2,1)S(1)} all-to-all(bf16[16,32,256]{2,1,0:T(8,128)(2,1)S(1)} %broadcast_in_dim.44), channel_id=1, replica_groups=mesh['grid'=16,'col'=2] {'grid'}, dimensions={0} | all-to-all | bytes 524288 | tf_op jit(solution)/shard_map/all_to_all | solution.py:397
  45.7 0.0 collective-permute-start.1
  45.7 1.5 collective-permute-done.1
  47.2 0.1 pad_maximum_fusion
  47.3 0.9 reverse_select_fusion
  48.2 29.0 %fit.2 = (bf16[9216,1024]{1,0:T(8,128)(2,1)}, bf16[32,3,96,256]{3,2,1,0:T(8,128)(2,1)}) custom-call(bf16[27648,256]{1,0:T(8,128)(2,1)} %orb_ref.3, bf16[1024,256]{1,0:T(8,128)(2,1)} %bitcast.24, bf16[1024,256]{1,0:T(8,128)(2,1)} %cinv_ref.3, bf16[96,288]{1,0:T(8,128)(2,1)} %constant.73.clone.table_ref), custom_call_target="tpu_custom_call" | custom-call | flops 12381585408 | bytes 28311552 | tf_op jit(solution)/shard_map/fit/pallas_call | solution.py:423
  77.2 3.6 all-to-all-start.2
  80.8 54.7 %fit.3 = (bf16[18432,1024]{1,0:T(8,128)(2,1)}, bf16[32,2,2,96,256]{4,3,2,1,0:T(8,128)(2,1)}, bf16[32,2,96,256]{3,2,1,0:T(8,128)(2,1)}) custom-call(bf16[27648,256]{1,0:T(8,128)(2,1)} %orb_ref.3, bf16[1024,256]{1,0:T(8,128)(2,1)} %bitcast.25, bf16[1024,256]{1,0:T(8,128)(2,1)} %cinv_ref.3, bf16[96,288]{1,0:T(8,128)(2,1)} %constant.73.clone.table_ref, ...), custom_call_target="tpu_custom_call" | custom-call | flops 24763170816 | bytes 56623104 | tf_op jit(solution)/shard_map/fit/pallas_call | solution.py:423
  135.5 50.4 %all-to-all-done.2.rest_0_ = bf16[32,3,96,256]{3,2,1,0:T(8,128)(2,1)} async-done(((bf16[32,3,96,256]{3,2,1,0:T(8,128)(2,1)}), bf16[32,3,96,256]{3,2,1,0:T(8,128)(2,1)}, u32[]{:S(2)}, u32[]{:S(2)}) %all-to-all-start.2) | async-done | bytes 4718624 | tf_op jit(solution)/shard_map/all_to_all | solution.py:376
  186.0 142.5 %all_to_all.47.rest_1_ = bf16[32,2,2,96,256]{4,3,2,1,0:T(8,128)(2,1)} all-to-all(bf16[32,2,2,96,256]{4,3,2,1,0:T(8,128)(2,1)} %get-tuple-element.29), channel_id=1, replica_groups=mesh['grid'=16,'col'=2] {'grid','col'}, dimensions={0} | all-to-all | bytes 12582912 | tf_op jit(solution)/shard_map/all_to_all | solution.py:376
  328.5 0.0 copy-start
  328.5 3.8 all-to-all-start.4
  332.3 0.0 copy-done
  332.3 0.6 dynamic_slice.17.wave_c_ref
  332.9 44.2 %solve.2 = (bf16[32,2,2,96,256]{4,3,2,1,0:T(8,128)(2,1)}, bf16[32,3,96,256]{3,2,1,0:T(8,128)(2,1)}) custom-call(f32[96]{0:T(128)} %constant.78.clone.wave_b_ref, f32[3]{0:T(128)} %dynamic_slice.17.wave_c_ref, f32[96,256]{1,0:T(8,128)} %constant.79.clone.wave_a_ref, bf16[96,192]{1,0:T(8,128)(2,1)} %constant.76.clone.table_ref, ...), custom_call_target="tpu_custom_call" | custom-call | flops 5435817984 | bytes 18874368 | tf_op jit(solution)/shard_map/solve/pallas_call | solution.py:470
  377.1 26.5 %all-to-all-done.4.rest_1_ = bf16[32,2,96,256]{3,2,1,0:T(8,128)(2,1)} async-done(((bf16[32,2,96,256]{3,2,1,0:T(8,128)(2,1)}), bf16[32,2,96,256]{3,2,1,0:T(8,128)(2,1)}, u32[]{:S(2)}, u32[]{:S(2)}) %all-to-all-start.4) | async-done | bytes 3145760 | tf_op jit(solution)/shard_map/all_to_all | solution.py:376
  403.6 4.3 all-to-all-start.5
  408.0 72.2 %spectrum.1 = (bf16[1024,9216]{1,0:T(8,128)(2,1)}, bf16[96,1024]{1,0:T(8,128)(2,1)}) custom-call(bf16[96,192]{1,0:T(8,128)(2,1)} %constant.72.clone.exact_ref, bf16[96,288]{1,0:T(8,128)(2,1)} %constant.73.clone.table_ref, bf16[18432,1024]{1,0:T(8,128)(2,1)} %get-tuple-element.34.pair_ref.rest_4_), custom_call_target="tpu_custom_call" | custom-call | flops 10871635968 | bytes 37748736 | tf_op jit(solution)/shard_map/spectrum/pallas_call | solution.py:498
  480.1 24.4 %solve.3 = (bf16[32,2,96,256]{3,2,1,0:T(8,128)(2,1)}, bf16[32,3,96,256]{3,2,1,0:T(8,128)(2,1)}) custom-call(f32[96]{0:T(128)} %constant.78.clone.wave_b_ref, f32[3]{0:T(128)} %dynamic_slice.17.wave_c_ref, f32[96,256]{1,0:T(8,128)} %constant.79.clone.wave_a_ref, bf16[96,192]{1,0:T(8,128)(2,1)} %constant.76.clone.table_ref, ...), custom_call_target="tpu_custom_call", output_to_operand_aliasing={{1}: (7, {})} | custom-call | flops 2717908992 | bytes 9437184 | tf_op jit(solution)/shard_map/solve/pallas_call | solution.py:470
  504.6 43.1 %all-to-all-done.5.rest_0_ = bf16[32,2,2,96,256]{4,3,2,1,0:T(8,128)(2,1)} async-done(((bf16[32,2,2,96,256]{4,3,2,1,0:T(8,128)(2,1)}), bf16[32,2,2,96,256]{4,3,2,1,0:T(8,128)(2,1)}, u32[]{:S(2)}, u32[]{:S(2)}) %all-to-all-start.5) | async-done | bytes 6291488 | tf_op jit(solution)/shard_map/all_to_all | solution.py:376
  547.6 74.7 %all_to_all.48.rest_1_ = bf16[32,2,96,256]{3,2,1,0:T(8,128)(2,1)} all-to-all(bf16[32,2,96,256]{3,2,1,0:T(8,128)(2,1)} %get-tuple-element.40), channel_id=1, replica_groups=mesh['grid'=16,'col'=2] {'grid','col'}, dimensions={0} | all-to-all | bytes 6291456 | tf_op jit(solution)/shard_map/all_to_all | solution.py:376
  622.3 3.7 all-to-all-start.7
  626.0 22.8 %couple.3 = (bf16[256,27648]{1,0:T(8,128)(2,1)}, f32[256,1024]{1,0:T(8,128)}) custom-call(bf16[32,2,2,96,256]{4,3,2,1,0:T(8,128)(2,1)} %all-to-all-done.5.rest_0_, bf16[32,2,96,256]{3,2,1,0:T(8,128)(2,1)} %all_to_all.48.rest_1_, bf16[96,192]{1,0:T(8,128)(2,1)} %constant.74.clone.rest_2_.rest_1_, bf16[96,288]{1,0:T(8,128)(2,1)} %constant.75.clone.rest_3_.rest_2_, ...), custom_call_target="tpu_custom_call" | custom-call | flops 7549747200 | bytes 28311552 | tf_op jit(solution)/shard_map/couple/pallas_call | solution.py:600
  648.8 23.0 %couple.4 = (bf16[256,27648]{1,0:T(8,128)(2,1)}, f32[256,1024]{1,0:T(8,128)}) custom-call(bf16[32,2,2,96,256]{4,3,2,1,0:T(8,128)(2,1)} %all-to-all-done.5.rest_0_, bf16[32,2,96,256]{3,2,1,0:T(8,128)(2,1)} %all_to_all.48.rest_1_, bf16[96,192]{1,0:T(8,128)(2,1)} %constant.74.clone.rest_2_.rest_1_, ...), custom_call_target="tpu_custom_call", output_to_operand_aliasing={{0}: (6, {})} | custom-call | flops 7549747200 | bytes 28311552 | tf_op jit(solution)/shard_map/couple/pallas_call | solution.py:600
  671.8 59.3 %all-to-all-done.7.rest_0_ = bf16[32,3,96,256]{3,2,1,0:T(8,128)(2,1)} async-done(((bf16[32,3,96,256]{3,2,1,0:T(8,128)(2,1)}), bf16[32,3,96,256]{3,2,1,0:T(8,128)(2,1)}, u32[]{:S(2)}, u32[]{:S(2)}) %all-to-all-start.7) | async-done | bytes 4718624 | tf_op jit(solution)/shard_map/all_to_all | solution.py:376
  731.1 15.7 %contract.1 = f32[1024,256]{1,0:T(8,128)} custom-call(f32[256,1024]{1,0:T(8,128)} %get-tuple-element.44.before_ref, bf16[96,1024]{1,0:T(8,128)(2,1)} %get-tuple-element.45.low_ref, bf16[1024,9216]{1,0:T(8,128)(2,1)} %get-tuple-element.46.left_ref, bf16[9216,256]{1,0:T(8,128)(2,1)} %bitcast.7.right_ref), custom_call_target="tpu_custom_call" | custom-call | flops 4831838208 | bytes 23592960 | tf_op jit(solution)/shard_map/contract/pallas_call | solution.py:547
  746.8 1.1 dynamic-slice_bitcast_fusion
  747.9 0.1 collective-permute-start.2
  748.0 1.9 collective-permute-done.2
  749.9 1.9 bitcast_add_fusion.rest_4_
  751.8 5.0 all-to-all-start.8
  756.8 0.6 broadcast_in_dim.45.rest_3_
  757.4 14.3 %couple.5 = bf16[256,27648]{1,0:T(8,128)(2,1)} custom-call(bf16[32,3,96,256]{3,2,1,0:T(8,128)(2,1)} %all-to-all-done.7.rest_0_, bf16[96,192]{1,0:T(8,128)(2,1)} %constant.74.clone.rest_2_.rest_1_, bf16[96,288]{1,0:T(8,128)(2,1)} %constant.75.clone.rest_3_.rest_2_, bf16[16,128]{1,0:T(8,128)(2,1)} %broadcast_in_dim.45.rest_3_, ...), custom_call_target="tpu_custom_call", output_to_operand_aliasing={{}: (5, {})} | custom-call | flops 7549747200 | bytes 28311552 | tf_op jit(solution)/shard_map/couple/pallas_call | solution.py:598
  771.7 0.5 all-to-all-done.8
  772.2 1.7 reduce_sum.22
  (4 shorter events, 0.1 us)
Async XLA Ops:
  12.9 1.7 collective-permute-start
  45.7 1.5 collective-permute-start.1
  77.2 108.7 %all-to-all-start.2 = ((bf16[32,3,96,256]{3,2,1,0:T(8,128)(2,1)}), bf16[32,3,96,256]{3,2,1,0:T(8,128)(2,1)}, u32[]{:S(2)}, u32[]{:S(2)}) async-start(bf16[32,3,96,256]{3,2,1,0:T(8,128)(2,1)} %get-tuple-element.25), calls=%async_computation.2 | async-start | bytes 9437184 | tf_op jit(solution)/shard_map/all_to_all | solution.py:376
  328.5 3.8 copy-start
  328.5 75.2 %all-to-all-start.4 = ((bf16[32,2,96,256]{3,2,1,0:T(8,128)(2,1)}), bf16[32,2,96,256]{3,2,1,0:T(8,128)(2,1)}, u32[]{:S(2)}, u32[]{:S(2)}) async-start(bf16[32,2,96,256]{3,2,1,0:T(8,128)(2,1)} %get-tuple-element.30), calls=%async_computation.4 | async-start | bytes 6291456 | tf_op jit(solution)/shard_map/all_to_all | solution.py:376
  403.6 144.0 %all-to-all-start.5 = ((bf16[32,2,2,96,256]{4,3,2,1,0:T(8,128)(2,1)}), bf16[32,2,2,96,256]{4,3,2,1,0:T(8,128)(2,1)}, u32[]{:S(2)}, u32[]{:S(2)}) async-start(bf16[32,2,2,96,256]{4,3,2,1,0:T(8,128)(2,1)} %get-tuple-element.39), calls=%async_computation.5 | async-start | bytes 12582912 | tf_op jit(solution)/shard_map/all_to_all | solution.py:376
  622.3 108.8 %all-to-all-start.7 = ((bf16[32,3,96,256]{3,2,1,0:T(8,128)(2,1)}), bf16[32,3,96,256]{3,2,1,0:T(8,128)(2,1)}, u32[]{:S(2)}, u32[]{:S(2)}) async-start(bf16[32,3,96,256]{3,2,1,0:T(8,128)(2,1)} %get-tuple-element.41), calls=%async_computation.7 | async-start | bytes 9437184 | tf_op jit(solution)/shard_map/all_to_all | solution.py:376
  747.9 2.0 collective-permute-start.2
  751.8 20.5 %all-to-all-start.8 = ((f32[16,32,256]{2,1,0:T(8,128)}), f32[16,32,256]{2,1,0:T(8,128)}, u32[]{:S(2)}, u32[]{:S(2)}) async-start(f32[16,32,256]{2,1,0:T(8,128)} %bitcast_add_fusion.rest_4_), calls=%async_computation.8 | async-start | bytes 1048576 | tf_op jit(solution)/shard_map/all_to_all | solution.py:602
